TPU v7x, 128 devices: a whole 4x4x4 slice. The times are simulated.
128 devices in a mesh: dp: 4 (over x), fy: 4 (over z_hi, core), fx: 8 (over z_lo, y).
Axes of the slice: x: 4, y: 4, z: 4 (z_hi: 2, z_lo: 2; z = z_hi * 2 + z_lo), core: 2. Of those that a mesh axis runs over, the one named last changes fastest.
Arguments:
- fine_tokens: bfloat16 [4, 64, 256, 768], P('dp', 'fy', 'fx'), may hold values from -40 to 40
- parent: int32 [4, 64, 64], P('dp', 'fy', 'fx'), may hold values from 0 to 511, as said below
- coarse_tokens: bfloat16 [4, 512, 768], P('dp', 'fx'), may hold values from -6 to 6
- tile_level: int32 [4, 512], P('dp', 'fx'), may hold values from 0 to 2
- level_table: float32 [3, 768], replicated, may hold values from -3 to 3
- norm_gain: float32 [768], replicated, may hold values from 0.5 to 1.5
- qkv_weight: bfloat16 [768, 2304], replicated, may hold values from -7 to 7
- out_weight: bfloat16 [768, 768], replicated, may hold values from -0.21875 to 0.21875
- cotangent: bfloat16 [4, 64, 256, 768], P('dp', 'fy', 'fx'), may hold values from -6 to 6
Outputs:
- mixed: bfloat16 [4, 64, 256, 768], P('dp', 'fy', 'fx')
- grad_tokens: bfloat16 [4, 64, 256, 768], P('dp', 'fy', 'fx')
- grad_coarse: float32 [4, 512, 768], P('dp', 'fx')
- grad_qkv: float32 [768, 2304], P('dp')
- grad_out: float32 [768, 768], P('dp')
- grad_gain: float32 [768], P('dp')
- grad_level: float32 [3, 768], replicated
Inputs may be any that keep to these rules, and one draw needn't show every extreme that they name: `parent`: each entry names a coarse token of the same frame; a token of level l is drawn with weight l + 1.
All inputs are finite; a program needn't handle non-finite values.
Results may differ from a plain program's by a relative error of at most 0.025.
Values may be sent and summed in bfloat16 or wider, within the bound.
A program may use at most 128 MiB of HBM per device.

v0:
```python
import functools
import math
import jax
import jax.numpy as jnp
from jax import lax
from jax.sharding import PartitionSpec as P

HEADS = 12
BLK = 4
LEVELS = 3


def as_sent(shard):
    return jax.tree.map(lambda a: a.astype(jnp.bfloat16) if a.dtype == jnp.float32 else a, shard)


def attend_forward(queries, key_rows, values, score_scale, query_form, key_form, score_form):
    scores = (
        jnp.einsum(
            query_form + "," + key_form + "->" + score_form,
            queries,
            key_rows,
            preferred_element_type=jnp.float32,
        )
        * score_scale
    )
    weights = jax.nn.softmax(scores, axis=-1)
    rounded = weights.astype(jnp.bfloat16)
    attended = jnp.einsum(
        score_form + "," + key_form + "->" + query_form,
        rounded,
        values,
        preferred_element_type=jnp.float32,
    )
    return attended.astype(jnp.bfloat16)


def attend_grads(
    weights,
    rounded,
    queries,
    key_rows,
    values,
    grad_out,
    score_scale,
    query_form,
    key_form,
    score_form,
):
    grad_values = jnp.einsum(
        score_form + "," + query_form + "->" + key_form,
        rounded,
        grad_out,
        preferred_element_type=jnp.float32,
    ).astype(jnp.bfloat16)
    grad_weights = jnp.einsum(
        query_form + "," + key_form + "->" + score_form,
        grad_out,
        values,
        preferred_element_type=jnp.float32,
    )
    inner = jnp.sum(weights * grad_weights, axis=-1, keepdims=True)
    grad_scores = (weights * (grad_weights - inner) * score_scale).astype(jnp.bfloat16)
    grad_queries = jnp.einsum(
        score_form + "," + key_form + "->" + query_form,
        grad_scores,
        key_rows,
        preferred_element_type=jnp.float32,
    ).astype(jnp.bfloat16)
    grad_keys = jnp.einsum(
        score_form + "," + query_form + "->" + key_form,
        grad_scores,
        queries,
        preferred_element_type=jnp.float32,
    ).astype(jnp.bfloat16)
    return (grad_queries, grad_keys, grad_values)


def attend_backward(
    queries, key_rows, values, grad_out, score_scale, query_form, key_form, score_form
):
    scores = (
        jnp.einsum(
            query_form + "," + key_form + "->" + score_form,
            queries,
            key_rows,
            preferred_element_type=jnp.float32,
        )
        * score_scale
    )
    weights = jax.nn.softmax(scores, axis=-1)
    rounded = weights.astype(jnp.bfloat16)
    return attend_grads(
        weights,
        rounded,
        queries,
        key_rows,
        values,
        grad_out,
        score_scale,
        query_form,
        key_form,
        score_form,
    )


def take_rows(table_rows, row_ids):
    return jnp.take(table_rows, row_ids, axis=0)


def rows_to_batch(tensor, head_dim):
    return tensor.reshape(tensor.shape[1], tensor.shape[2], -1, head_dim)


def batch_to_rows(tensor):
    return tensor.reshape(1, tensor.shape[0], tensor.shape[1], -1)


def columns_to_batch(tensor, head_dim):
    return tensor.reshape(tensor.shape[0], tensor.shape[1], tensor.shape[3], -1, head_dim)


def batch_to_columns(tensor):
    return tensor.reshape(tensor.shape[0], tensor.shape[1], 1, tensor.shape[2], -1)


def to_row_groups(tensor, groups):
    return tensor.reshape(groups, -1, tensor.shape[2], tensor.shape[3])


def to_column_groups(tensor, groups):
    return tensor.reshape(tensor.shape[0], tensor.shape[1], groups, -1, tensor.shape[3])


def local(
    fine_tokens,
    parent,
    coarse_tokens,
    tile_level,
    level_table,
    norm_gain,
    qkv_weight,
    out_weight,
    cotangent,
):
    frame_count, row_count, column_count, model_dim = fine_tokens.shape
    row_groups = lax.axis_size("fx")
    column_groups = lax.axis_size("fy")
    owners_dev = coarse_tokens.shape[1]
    half_width = model_dim // 2
    head_dim = model_dim // HEADS
    score_scale = head_dim ** (-0.5)
    block_count = column_count // BLK
    token_shape = (frame_count, row_count, column_count, half_width)
    level_onehot = (tile_level[:, :, None] == jnp.arange(LEVELS, dtype=jnp.int32)).astype(
        jnp.float32
    )
    level_add = jnp.sum(level_onehot[:, :, :, None] * level_table[None, None, :, :], axis=2)
    summary = (coarse_tokens.astype(jnp.float32) + level_add).astype(jnp.bfloat16)
    shard_piece = lax.all_gather(summary, "fx", axis=1, tiled=True)
    piece_rows = shard_piece.shape[1]
    inside = (parent >= 0) & (parent < piece_rows)
    local_index = jnp.clip(parent, 0, piece_rows - 1)
    picked = jax.vmap(take_rows)(shard_piece, local_index)
    read_rows = jnp.where(inside[..., None], picked.astype(jnp.float32), 0.0)
    spread = jnp.broadcast_to(
        read_rows[:, :, :, None, :], (frame_count, row_count, block_count, BLK, model_dim)
    )
    residual = fine_tokens.astype(jnp.float32) + spread.reshape(
        frame_count, row_count, column_count, model_dim
    )
    inv_rms = lax.rsqrt(jnp.mean(residual * residual, axis=-1, keepdims=True) + 1e-06)
    normed_pre = residual * inv_rms
    normed = (normed_pre * norm_gain).astype(jnp.bfloat16)
    flat_normed = normed.reshape(-1, model_dim)
    projected = jnp.dot(flat_normed, qkv_weight, preferred_element_type=jnp.float32).astype(
        jnp.bfloat16
    )
    projected = projected.reshape(frame_count, row_count, column_count, 3 * model_dim)
    row_query = projected[..., 0:half_width]
    column_query = projected[..., half_width:model_dim]
    row_key = projected[..., model_dim : model_dim + half_width]
    column_key = projected[..., model_dim + half_width : 2 * model_dim]
    row_value = projected[..., 2 * model_dim : 2 * model_dim + half_width]
    column_value = projected[..., 2 * model_dim + half_width : 3 * model_dim]
    flat_cot = cotangent.reshape(-1, model_dim)
    grad_att = jnp.dot(flat_cot, out_weight.T, preferred_element_type=jnp.float32).astype(
        jnp.bfloat16
    )
    grad_att = grad_att.reshape(frame_count, row_count, column_count, model_dim)
    row_grad_out = grad_att[..., 0:half_width]
    column_grad_out = grad_att[..., half_width:model_dim]
    queries = lax.all_to_all(
        to_row_groups(row_query, row_groups), "fx", split_axis=0, concat_axis=2, tiled=True
    )
    key_rows = lax.all_to_all(
        to_row_groups(row_key, row_groups), "fx", split_axis=0, concat_axis=2, tiled=True
    )
    values = lax.all_to_all(
        to_row_groups(row_value, row_groups), "fx", split_axis=0, concat_axis=2, tiled=True
    )
    attended_rows = attend_forward(
        rows_to_batch(queries, head_dim),
        rows_to_batch(key_rows, head_dim),
        rows_to_batch(values, head_dim),
        score_scale,
        "bqhd",
        "bkhd",
        "bhqk",
    )
    row_out = lax.all_to_all(
        batch_to_rows(attended_rows), "fx", split_axis=2, concat_axis=0, tiled=True
    )
    row_out = row_out.reshape(token_shape)
    queries = lax.all_to_all(
        to_column_groups(column_query, column_groups), "fy", split_axis=2, concat_axis=1, tiled=True
    )
    key_rows = lax.all_to_all(
        to_column_groups(column_key, column_groups), "fy", split_axis=2, concat_axis=1, tiled=True
    )
    values = lax.all_to_all(
        to_column_groups(column_value, column_groups), "fy", split_axis=2, concat_axis=1, tiled=True
    )
    attended_columns = attend_forward(
        columns_to_batch(queries, head_dim),
        columns_to_batch(key_rows, head_dim),
        columns_to_batch(values, head_dim),
        score_scale,
        "fqchd",
        "fkchd",
        "fchqk",
    )
    column_out = lax.all_to_all(
        batch_to_columns(attended_columns), "fy", split_axis=1, concat_axis=2, tiled=True
    )
    column_out = column_out.reshape(token_shape)
    queries = lax.all_to_all(
        to_row_groups(row_query, row_groups), "fx", split_axis=0, concat_axis=2, tiled=True
    )
    key_rows = lax.all_to_all(
        to_row_groups(row_key, row_groups), "fx", split_axis=0, concat_axis=2, tiled=True
    )
    values = lax.all_to_all(
        to_row_groups(row_value, row_groups), "fx", split_axis=0, concat_axis=2, tiled=True
    )
    grad_rows = lax.all_to_all(
        to_row_groups(row_grad_out, row_groups), "fx", split_axis=0, concat_axis=2, tiled=True
    )
    grads = attend_backward(
        rows_to_batch(queries, head_dim),
        rows_to_batch(key_rows, head_dim),
        rows_to_batch(values, head_dim),
        rows_to_batch(grad_rows, head_dim),
        score_scale,
        "bqhd",
        "bkhd",
        "bhqk",
    )
    row_back = (
        lax.all_to_all(batch_to_rows(grads[0]), "fx", split_axis=2, concat_axis=0, tiled=True),
        lax.all_to_all(batch_to_rows(grads[1]), "fx", split_axis=2, concat_axis=0, tiled=True),
        lax.all_to_all(batch_to_rows(grads[2]), "fx", split_axis=2, concat_axis=0, tiled=True),
    )
    queries = lax.all_to_all(
        to_column_groups(column_query, column_groups), "fy", split_axis=2, concat_axis=1, tiled=True
    )
    key_rows = lax.all_to_all(
        to_column_groups(column_key, column_groups), "fy", split_axis=2, concat_axis=1, tiled=True
    )
    values = lax.all_to_all(
        to_column_groups(column_value, column_groups), "fy", split_axis=2, concat_axis=1, tiled=True
    )
    grad_columns = lax.all_to_all(
        to_column_groups(column_grad_out, column_groups),
        "fy",
        split_axis=2,
        concat_axis=1,
        tiled=True,
    )
    grads = attend_backward(
        columns_to_batch(queries, head_dim),
        columns_to_batch(key_rows, head_dim),
        columns_to_batch(values, head_dim),
        columns_to_batch(grad_columns, head_dim),
        score_scale,
        "fqchd",
        "fkchd",
        "fchqk",
    )
    column_back = (
        lax.all_to_all(batch_to_columns(grads[0]), "fy", split_axis=1, concat_axis=2, tiled=True),
        lax.all_to_all(batch_to_columns(grads[1]), "fy", split_axis=1, concat_axis=2, tiled=True),
        lax.all_to_all(batch_to_columns(grads[2]), "fy", split_axis=1, concat_axis=2, tiled=True),
    )
    attended = jnp.concatenate([row_out, column_out], axis=-1)
    flat_att = attended.reshape(-1, model_dim)
    out_proj = jnp.dot(flat_att, out_weight, preferred_element_type=jnp.float32)
    mixed = (residual + out_proj.reshape(frame_count, row_count, column_count, model_dim)).astype(
        jnp.bfloat16
    )
    grad_out_local = jnp.dot(flat_att.T, flat_cot, preferred_element_type=jnp.float32)
    pieces = []
    for which in range(3):
        pieces.append(row_back[which].reshape(token_shape))
        pieces.append(column_back[which].reshape(token_shape))
    grad_projected = jnp.concatenate(pieces, axis=-1).reshape(-1, 3 * model_dim)
    grad_normed = jnp.dot(grad_projected, qkv_weight.T, preferred_element_type=jnp.float32)
    grad_qkv_local = jnp.dot(flat_normed.T, grad_projected, preferred_element_type=jnp.float32)
    flat_pre = normed_pre.reshape(-1, model_dim)
    grad_gain_local = jnp.sum(grad_normed * flat_pre, axis=0)
    grad_pre = grad_normed * norm_gain
    flat_inv = inv_rms.reshape(-1, 1)
    grad_residual = flat_inv * (
        grad_pre - flat_pre * jnp.mean(grad_pre * flat_pre, axis=-1, keepdims=True)
    ) + flat_cot.astype(jnp.float32)
    grad_fine = grad_residual.astype(jnp.bfloat16).reshape(
        frame_count, row_count, column_count, model_dim
    )
    block_grad = (
        grad_residual.reshape(frame_count, row_count, block_count, BLK, model_dim)
        .sum(axis=3)
        .reshape(frame_count, -1, model_dim)
    )
    parent_flat = parent.reshape(frame_count, -1)
    coarse_total = owners_dev * row_groups
    segment_rows = functools.partial(jax.ops.segment_sum, num_segments=coarse_total)
    dense_sum = jax.vmap(segment_rows)(block_grad, parent_flat)
    owned_rows = jax.tree.map(
        lambda part: part.astype(jnp.float32),
        lax.psum_scatter(as_sent(dense_sum), "fx", scatter_dimension=1, tiled=True),
    )
    grad_coarse = jax.tree.map(
        lambda part: part.astype(jnp.float32), lax.psum(as_sent(owned_rows), "fy")
    )
    level_part = jnp.sum(level_onehot[:, :, :, None] * grad_coarse[:, :, None, :], axis=(0, 1))
    grad_level = lax.psum(level_part, ("dp", "fx"))
    summed = (
        lax.psum(grad_qkv_local.astype(jnp.bfloat16), ("fy", "fx")).astype(jnp.float32),
        lax.psum(grad_out_local.astype(jnp.bfloat16), ("fy", "fx")).astype(jnp.float32),
        lax.psum(grad_gain_local.astype(jnp.bfloat16), ("fy", "fx")).astype(jnp.float32),
    )
    shares = (
        lax.psum_scatter(
            summed[0].astype(jnp.bfloat16), "dp", scatter_dimension=0, tiled=True
        ).astype(jnp.float32),
        lax.psum_scatter(
            summed[1].astype(jnp.bfloat16), "dp", scatter_dimension=0, tiled=True
        ).astype(jnp.float32),
        lax.psum_scatter(
            summed[2].astype(jnp.bfloat16), "dp", scatter_dimension=0, tiled=True
        ).astype(jnp.float32),
    )
    total_tokens = (
        frame_count * row_count * column_count * lax.axis_size("dp") * column_groups * row_groups
    )
    grad_scale = 1.0 / math.sqrt(total_tokens)
    return (
        mixed,
        grad_fine,
        grad_coarse,
        shares[0] * grad_scale,
        shares[1] * grad_scale,
        shares[2] * grad_scale,
        grad_level * grad_scale,
    )


def solution(mesh):
    return jax.shard_map(
        local,
        mesh=mesh,
        in_specs=(
            P("dp", "fy", "fx", None),
            P("dp", "fy", "fx"),
            P("dp", "fx", None),
            P("dp", "fx"),
            P(),
            P(),
            P(),
            P(),
            P("dp", "fy", "fx", None),
        ),
        out_specs=(
            P("dp", "fy", "fx", None),
            P("dp", "fy", "fx", None),
            P("dp", "fx", None),
            P("dp", None),
            P("dp", None),
            P("dp"),
            P(),
        ),
        check_vma=False,
    )
```

profile of v0, /device:TPU:0, one launch (start us, length us, event | category | flops | bytes accessed | tf_op | source)
XLA Modules:
  0.0 606.6 jit_solution(17159746881032802387)
XLA Ops:
  8.0 2.5 convolution_convert_fusion.1
  12.2 5.3 all-to-all-start.10
  23.4 31.8 %all_gather.3 = bf16[1,512,768]{2,1,0:T(8,128)(2,1)} all-gather(bf16[1,64,768]{2,1,0:T(8,128)(2,1)S(1)} %fusion.66), channel_id=1, replica_groups=mesh['dp'=4,'fy'=4,'fx'=8] {'fx'}, dimensions={1}, use_global_device_ids=true | all-gather | bytes 884736 | tf_op jit(solution)/shard_map/all_gather | solution.py:160
  55.2 2.8 gather_fusion
  60.5 2.8 broadcast_in_dim.39
  71.1 5.4 all-to-all-start.6
  78.3 7.2 %all-to-all-done.6 = bf16[1,16,4,8,384]{4,3,1,0,2:T(8,128)(2,1)} async-done(((bf16[1,16,4,8,384]{4,3,1,0,2:T(8,128)(2,1)}), bf16[1,16,4,8,384]{4,3,1,0,2:T(8,128)(2,1)}, u32[]{:S(2)}, u32[]{:S(2)}) %all-to-all-start.6) | async-done | bytes 393248 | tf_op jit(solution)/shard_map/all_to_all | solution.py:218
  85.5 4.1 all-to-all-start.5
  91.4 7.2 %all-to-all-done.5 = bf16[1,16,4,8,384]{4,3,1,0,2:T(8,128)(2,1)} async-done(((bf16[1,16,4,8,384]{4,3,1,0,2:T(8,128)(2,1)}), bf16[1,16,4,8,384]{4,3,1,0,2:T(8,128)(2,1)}, u32[]{:S(2)}, u32[]{:S(2)}) %all-to-all-start.5) | async-done | bytes 393248 | tf_op jit(solution)/shard_map/all_to_all | solution.py:215
  98.6 13.2 %all_to_all.270 = bf16[1,16,4,8,384]{4,3,1,0,2:T(8,128)(2,1)} all-to-all(bf16[1,16,4,8,384]{4,3,1,0,2:T(8,128)(2,1)} %copy.222), channel_id=1, replica_groups=mesh['dp'=4,'fy'=4,'fx'=8] {'fy'}, dimensions={2} | all-to-all | bytes 786432 | tf_op jit(solution)/shard_map/all_to_all | solution.py:221
  111.8 12.7 %all_to_all.271 = bf16[8,2,32,384]{3,2,1,0:T(8,128)(2,1)} all-to-all(bf16[8,2,32,384]{3,2,1,0:T(8,128)(2,1)} %bitcast.260), channel_id=1, replica_groups=mesh['dp'=4,'fy'=4,'fx'=8] {'fx'}, dimensions={0} | all-to-all | bytes 786432 | tf_op jit(solution)/shard_map/all_to_all | solution.py:246
  124.5 11.1 %all_to_all.272 = bf16[8,2,32,384]{3,2,1,0:T(8,128)(2,1)} all-to-all(bf16[8,2,32,384]{3,2,1,0:T(8,128)(2,1)S(1)} %bitcast.251), channel_id=1, replica_groups=mesh['dp'=4,'fy'=4,'fx'=8] {'fx'}, dimensions={0} | all-to-all | bytes 786432 | tf_op jit(solution)/shard_map/all_to_all | solution.py:196
  135.6 4.1 all-to-all-start.1
  139.7 2.4 reshape.396
  142.1 2.7 copy.260
  144.7 2.4 reshape.383
  147.1 2.5 reshape.385
  149.6 2.7 copy.251
  152.3 2.5 reshape.387
  154.7 2.7 copy.242
  157.4 3.3 fusion.59
  160.7 6.1 %all-to-all-start = ((bf16[8,2,32,384]{3,2,1,0:T(8,128)(2,1)}), bf16[8,2,32,384]{3,2,1,0:T(8,128)(2,1)}, u32[]{:S(2)}, u32[]{:S(2)}) async-start(bf16[8,2,32,384]{3,2,1,0:T(8,128)(2,1)} %bitcast.249), calls=%async_computation | async-start | bytes 786432 | tf_op jit(solution)/shard_map/all_to_all | solution.py:199
  166.9 4.0 fusion.89
  170.8 4.6 fusion.37
  175.4 2.2 copy.244
  177.6 4.1 all-to-all-start.11
  181.8 3.0 convolution_convert_fusion.2
  184.8 2.2 copy.262
  187.0 4.6 fusion.40
  191.7 2.2 copy.253
  193.9 2.7 copy.283
  196.6 3.0 reshape.446
  199.6 2.7 copy.279
  202.4 3.0 reshape.443
  205.4 2.7 copy.280
  208.1 3.0 reshape.444
  211.1 2.7 copy.281
  213.9 3.0 reshape.445
  216.9 4.8 all-to-all-start.13
  221.7 4.5 fusion.90
  226.2 4.5 all-to-all-done.13
  230.7 4.1 all-to-all-start.15
  234.8 3.3 convolution_convert_fusion.4
  240.1 3.7 all-to-all-done.15
  243.8 5.9 all-to-all-start.14
  249.7 3.4 fusion.91
  253.1 6.6 %fusion.43 = bf16[2,6,64,256]{3,2,1,0:T(8,128)(2,1)} fusion(bf16[2,256,6,64]{1,3,2,0:T(8,128)(2,1)} %reshape.445, f32[2,6,256,256]{2,3,1,0:T(8,128)} %fusion.91, f32[2,6,256,256]{2,3,1,0:T(8,128)} %get-tuple-element.28, f32[2,6,256]{2,1,0:T(8,128)} %get-tuple-element.27), kind=kOutput, calls=%fused_computation.49 | convolution fusion | flops 106368256 | bytes 7090176 | tf_op jit(solution)/shard_map/bhqk,bkhd->bqhd/dot_general | solution.py:64
  261.6 5.7 all-to-all-start.9
  267.3 6.6 %fusion.46 = bf16[2,6,64,256]{3,2,1,0:T(8,128)(2,1)} fusion(bf16[2,256,6,64]{1,3,2,0:T(8,128)(2,1)} %reshape.444, f32[2,6,256,256]{2,3,1,0:T(8,128)} %fusion.91, f32[2,6,256,256]{2,3,1,0:T(8,128)} %get-tuple-element.28, f32[2,6,256]{2,1,0:T(8,128)} %get-tuple-element.27), kind=kOutput, calls=%fused_computation.50 | convolution fusion | flops 106368256 | bytes 7090176 | tf_op jit(solution)/shard_map/bhqk,bqhd->bkhd/dot_general | solution.py:70
  275.8 5.7 all-to-all-start.12
  295.8 2.2 fusion.22
  304.1 2.1 convolution_convert_fusion.3
  307.3 3.5 all-to-all-start.7
  310.8 2.3 convolution_convert_fusion.5
  314.2 6.9 %all-to-all-done.7 = bf16[1,64,1,8,384]{4,3,2,0,1:T(8,128)(2,1)S(1)} async-done(((bf16[1,64,1,8,384]{4,3,2,0,1:T(8,128)(2,1)}), bf16[1,64,1,8,384]{4,3,2,0,1:T(8,128)(2,1)S(1)}, u32[]{:S(2)}, u32[]{:S(2)}) %all-to-all-start.7) | async-done | bytes 393248 | tf_op jit(solution)/shard_map/all_to_all | solution.py:233
  321.1 5.1 all-to-all-start.3
  326.3 9.3 %all-to-all-done.3 = bf16[1,2,256,384]{3,1,0,2:T(2,128)(2,1)S(1)} async-done(((bf16[1,2,256,384]{3,1,0,2:T(2,128)(2,1)}), bf16[1,2,256,384]{3,1,0,2:T(2,128)(2,1)S(1)}, u32[]{:S(2)}, u32[]{:S(2)}) %all-to-all-start.3) | async-done | bytes 393248 | tf_op jit(solution)/shard_map/all_to_all | solution.py:211
  337.6 6.4 %reduce-scatter.4.cloned.1.call-done = bf16[1,64,768]{2,1,0:T(8,128)(2,1)} async-done(((bf16[1,512,768]{2,1,0:T(8,128)(2,1)}), bf16[1,64,768]{2,1,0:T(8,128)(2,1)}) %reduce-scatter.4.cloned.1.call-update) | async-done | bytes 98320 | tf_op jit(solution)/shard_map/reduce_scatter | solution.py:330
  352.4 5.5 bitcast_convert_fusion
  359.8 10.5 %all-reduce = bf16[768]{0:T(1024)(128)(2,1)S(1)} all-reduce(bf16[768]{0:T(1024)(128)(2,1)S(1)} %get-tuple-element.7), channel_id=5, replica_groups=mesh['dp'=4,'fy'=4,'fx'=8] {'dp'}, use_global_device_ids=true, to_apply=%region_19.20.clone | all-reduce | flops 768 | bytes 3072
  370.4 62.7 %psum.42 = bf16[192]{0:T(256)(128)(2,1)S(1)} all-reduce(bf16[192]{0:T(256)(128)(2,1)S(1)} %dynamic-slice.1), channel_id=1, replica_groups=mesh['dp'=4,'fy'=4,'fx'=8] {'fy','fx'}, use_global_device_ids=true, to_apply=%region_18.19 | all-reduce | flops 192 | bytes 768 | tf_op jit(solution)/shard_map/psum | solution.py:340
  433.7 2.9 fusion.23
  439.3 154.4 %psum.39 = f32[3,768]{1,0:T(4,128)S(1)} all-reduce(f32[3,768]{1,0:T(4,128)S(1)} %multiply_reduce_fusion.4), channel_id=1, replica_groups=mesh['dp'=4,'fy'=4,'fx'=8] {'dp','fx'}, use_global_device_ids=true, to_apply=%region_21.22 | all-reduce | flops 2304 | bytes 18432 | tf_op jit(solution)/shard_map/psum | solution.py:336
  596.3 2.5 convert_multiply_fusion
  (153 shorter events, 67.3 us)
Async XLA Ops:
  8.0 59.0 %copy-start = (bf16[768,2304]{1,0:T(8,128)(2,1)S(1)}, bf16[768,2304]{1,0:T(8,128)(2,1)}, u32[]{:S(2)}) copy-start(bf16[768,2304]{1,0:T(8,128)(2,1)} %param.15) | copy-start | bytes 10616836
  10.5 7.0 %copy-start.23 = (s32[1,16,8]{1,2,0:T(8,128)S(1)}, s32[1,16,8]{1,2,0:T(8,128)}, u32[]{:S(2)}) copy-start(s32[1,16,8]{1,2,0:T(8,128)} %param.10) | copy-start | bytes 1540
  10.5 7.5 %copy-start.27 = (s32[1,64]{1,0:T(1,128)S(1)}, s32[1,64]{1,0:T(1,128)}, u32[]{:S(2)}) copy-start(s32[1,64]{1,0:T(1,128)} %param.12) | copy-start | bytes 772
  12.2 58.9 %all-to-all-start.10 = ((bf16[1,16,4,8,384]{4,3,1,0,2:T(8,128)(2,1)}), bf16[1,16,4,8,384]{4,3,1,0,2:T(8,128)(2,1)}, u32[]{:S(2)}, u32[]{:S(2)}) async-start(bf16[1,16,4,8,384]{4,3,1,0,2:T(8,128)(2,1)} %copy.239), calls=%async_computation.10 | async-start | bytes 786432 | tf_op jit(solution)/shard_map/all_to_all | solution.py:273
  63.3 2.1 copy-start.2
  63.3 2.3 copy-start.12
  63.3 2.3 copy-start.25
  67.0 2.0 copy-start.21
  71.1 14.4 %all-to-all-start.6 = ((bf16[1,16,4,8,384]{4,3,1,0,2:T(8,128)(2,1)}), bf16[1,16,4,8,384]{4,3,1,0,2:T(8,128)(2,1)}, u32[]{:S(2)}, u32[]{:S(2)}) async-start(bf16[1,16,4,8,384]{4,3,1,0,2:T(8,128)(2,1)} %copy.224), calls=%async_computation.6 | async-start | bytes 786432 | tf_op jit(solution)/shard_map/all_to_all | solution.py:218
  85.5 13.1 %all-to-all-start.5 = ((bf16[1,16,4,8,384]{4,3,1,0,2:T(8,128)(2,1)}), bf16[1,16,4,8,384]{4,3,1,0,2:T(8,128)(2,1)}, u32[]{:S(2)}, u32[]{:S(2)}) async-start(bf16[1,16,4,8,384]{4,3,1,0,2:T(8,128)(2,1)} %copy.223), calls=%async_computation.5 | async-start | bytes 786432 | tf_op jit(solution)/shard_map/all_to_all | solution.py:215
  98.6 25.9 %copy-start.14 = (bf16[1,16,32,384]{3,2,1,0:T(8,128)(2,1)S(1)}, bf16[1,16,32,384]{3,2,1,0:T(8,128)(2,1)}, u32[]{:S(2)}) copy-start(bf16[1,16,32,384]{3,2,1,0:T(8,128)(2,1)} %get-tuple-element.15) | copy-start | bytes 1179652
  135.6 25.2 %all-to-all-start.1 = ((bf16[8,2,32,384]{3,2,1,0:T(8,128)(2,1)}), bf16[8,2,32,384]{3,2,1,0:T(8,128)(2,1)}, u32[]{:S(2)}, u32[]{:S(2)}) async-start(bf16[8,2,32,384]{3,2,1,0:T(8,128)(2,1)} %bitcast.250), calls=%async_computation.1 | async-start | bytes 786432 | tf_op jit(solution)/shard_map/all_to_all | solution.py:193
  160.7 16.9 %all-to-all-start = ((bf16[8,2,32,384]{3,2,1,0:T(8,128)(2,1)}), bf16[8,2,32,384]{3,2,1,0:T(8,128)(2,1)}, u32[]{:S(2)}, u32[]{:S(2)}) async-start(bf16[8,2,32,384]{3,2,1,0:T(8,128)(2,1)} %bitcast.249), calls=%async_computation | async-start | bytes 786432 | tf_op jit(solution)/shard_map/all_to_all | solution.py:199
  177.6 39.3 %all-to-all-start.11 = ((bf16[1,64,1,8,384]{4,3,2,0,1:T(8,128)(2,1)}), bf16[1,64,1,8,384]{4,3,2,0,1:T(8,128)(2,1)}, u32[]{:S(2)}, u32[]{:S(2)}) async-start(bf16[1,64,1,8,384]{4,3,2,0,1:T(8,128)(2,1)} %copy.244), calls=%async_computation.11 | async-start | bytes 786432 | tf_op jit(solution)/shard_map/all_to_all | solution.py:291
  216.9 13.8 %all-to-all-start.13 = ((bf16[1,64,1,8,384]{4,3,2,0,1:T(8,128)(2,1)}), bf16[1,64,1,8,384]{4,3,2,0,1:T(8,128)(2,1)}, u32[]{:S(2)}, u32[]{:S(2)}) async-start(bf16[1,64,1,8,384]{4,3,2,0,1:T(8,128)(2,1)} %copy.253), calls=%async_computation.13 | async-start | bytes 786432 | tf_op jit(solution)/shard_map/all_to_all | solution.py:292
  230.7 13.1 %all-to-all-start.15 = ((bf16[1,64,1,8,384]{4,3,2,0,1:T(8,128)(2,1)}), bf16[1,64,1,8,384]{4,3,2,0,1:T(8,128)(2,1)}, u32[]{:S(2)}, u32[]{:S(2)}) async-start(bf16[1,64,1,8,384]{4,3,2,0,1:T(8,128)(2,1)} %copy.262), calls=%async_computation.15 | async-start | bytes 786432 | tf_op jit(solution)/shard_map/all_to_all | solution.py:293
  243.8 17.8 %all-to-all-start.14 = ((bf16[1,2,256,384]{3,1,0,2:T(2,128)(2,1)}), bf16[1,2,256,384]{3,1,0,2:T(2,128)(2,1)}, u32[]{:S(2)}, u32[]{:S(2)}) async-start(bf16[1,2,256,384]{3,1,0,2:T(2,128)(2,1)} %copy.257), calls=%async_computation.14 | async-start | bytes 786432 | tf_op jit(solution)/shard_map/all_to_all | solution.py:262
  261.6 14.2 %all-to-all-start.9 = ((bf16[1,2,256,384]{3,1,0,2:T(2,128)(2,1)}), bf16[1,2,256,384]{3,1,0,2:T(2,128)(2,1)}, u32[]{:S(2)}, u32[]{:S(2)}) async-start(bf16[1,2,256,384]{3,1,0,2:T(2,128)(2,1)} %copy.236), calls=%async_computation.9 | async-start | bytes 786432 | tf_op jit(solution)/shard_map/all_to_all | solution.py:260
  275.8 16.9 %all-to-all-start.12 = ((bf16[1,2,256,384]{3,1,0,2:T(2,128)(2,1)}), bf16[1,2,256,384]{3,1,0,2:T(2,128)(2,1)}, u32[]{:S(2)}, u32[]{:S(2)}) async-start(bf16[1,2,256,384]{3,1,0,2:T(2,128)(2,1)} %copy.248), calls=%async_computation.12 | async-start | bytes 786432 | tf_op jit(solution)/shard_map/all_to_all | solution.py:261
  281.6 62.5 %reduce-scatter.4.cloned.1.call-start = ((), (), s32[]{:S(2)}) async-start(), calls=%async_computation.19 | async-start | bytes 884736 | tf_op jit(solution)/shard_map/reduce_scatter | solution.py:330
  292.7 1.2 copy-start.9
  292.7 1.3 copy-start.17
  293.8 1.1 copy-start.16
  293.9 1.1 copy-start.7
  293.9 1.2 copy-start.5
  294.0 1.2 copy-start.15
  294.1 1.7 copy-start.4
  294.1 1.7 copy-start.26
  295.8 2.2 copy-start.19
  302.6 1.5 copy-start.11
  302.6 1.5 copy-start.24
  306.2 4.6 copy-start.18
  306.2 4.6 copy-start.29
  307.3 13.8 %all-to-all-start.7 = ((bf16[1,64,1,8,384]{4,3,2,0,1:T(8,128)(2,1)}), bf16[1,64,1,8,384]{4,3,2,0,1:T(8,128)(2,1)S(1)}, u32[]{:S(2)}, u32[]{:S(2)}) async-start(bf16[1,64,1,8,384]{4,3,2,0,1:T(8,128)(2,1)} %copy.229), calls=%async_computation.7 | async-start | bytes 786432 | tf_op jit(solution)/shard_map/all_to_all | solution.py:233
  314.2 21.5 %copy-start.20 = (bf16[1,16,32,768]{3,2,1,0:T(8,128)(2,1)S(1)}, bf16[1,16,32,768]{3,2,1,0:T(8,128)(2,1)}, u32[]{:S(2)}) copy-start(bf16[1,16,32,768]{3,2,1,0:T(8,128)(2,1)} %param.17) | copy-start | bytes 2359300
  321.1 14.5 %all-to-all-start.3 = ((bf16[1,2,256,384]{3,1,0,2:T(2,128)(2,1)}), bf16[1,2,256,384]{3,1,0,2:T(2,128)(2,1)S(1)}, u32[]{:S(2)}, u32[]{:S(2)}) async-start(bf16[1,2,256,384]{3,1,0,2:T(2,128)(2,1)} %copy.219), calls=%async_computation.3 | async-start | bytes 786432 | tf_op jit(solution)/shard_map/all_to_all | solution.py:211
  326.2 110.4 %all-reduce.5.cloned.1.call-start = ((), (), s32[]{:S(2)}) async-start(), calls=%async_computation.20 | async-start | bytes 196608 | tf_op jit(solution)/shard_map/psum | solution.py:333
  335.8 8.3 %copy-start.10 = (bf16[8,1,2,32,384]{4,3,2,0,1:T(8,128)(2,1)S(1)}, bf16[8,1,2,32,384]{4,3,2,0,1:T(8,128)(2,1)}, u32[]{:S(2)}) copy-start(bf16[8,1,2,32,384]{4,3,2,0,1:T(8,128)(2,1)} %copy.238) | copy-start | bytes 1179652
  337.6 9.5 %copy-start.8 = (bf16[8,1,2,32,384]{4,3,2,0,1:T(8,128)(2,1)S(1)}, bf16[8,1,2,32,384]{4,3,2,0,1:T(8,128)(2,1)}, u32[]{:S(2)}) copy-start(bf16[8,1,2,32,384]{4,3,2,0,1:T(8,128)(2,1)} %copy-done.7) | copy-start | bytes 1179652
  344.0 94.2 %reduce-scatter.8.cloned.1.call-start = ((), (), s32[]{:S(2)}) async-start(), calls=%async_computation.22 | async-start | bytes 1474560 | tf_op jit(solution)/shard_map/reduce_scatter | solution.py:346
  345.0 4.8 copy-start.6
  345.0 93.2 %reduce-scatter.6.cloned.1.call-start = ((), (), s32[]{:S(2)}) async-start(), calls=%async_computation.21 | async-start | bytes 4423680 | tf_op jit(solution)/shard_map/reduce_scatter | solution.py:343
  347.1 5.3 copy-start.22
  357.9 0.7 copy-start.28
  357.9 75.8 %copy-start.3 = (f32[1,16,32,768]{3,2,1,0:T(8,128)S(1)}, f32[1,16,32,768]{3,2,1,0:T(8,128)}, u32[]{:S(2)}) copy-start(f32[1,16,32,768]{3,2,1,0:T(8,128)} %broadcast_in_dim.39) | copy-start | bytes 4718596
  357.9 75.8 %copy-start.13 = (bf16[1,16,32,768]{3,2,1,0:T(8,128)(2,1)S(1)}, bf16[1,16,32,768]{3,2,1,0:T(8,128)(2,1)}, u32[]{:S(2)}) copy-start(bf16[1,16,32,768]{3,2,1,0:T(8,128)(2,1)} %param.9) | copy-start | bytes 2359300
  357.9 236.4 %all-reduce.7.cloned.1.call-start = ((), (), s32[]{:S(2)}) async-start(), calls=%async_computation.23 | async-start | bytes 2359296 | tf_op jit(solution)/shard_map/psum | solution.py:338
  594.3 4.5 copy-start.1
Sparse Core Ops, SparseCore 0:
  303.7 40.2 reduce-scatter.3
  346.5 38.8 all-reduce.4
Sparse Core Ops, SparseCore 1:
  347.5 23.0 reduce-scatter.7
  372.9 41.1 reduce-scatter.5
  438.3 101.2 all-reduce.6
where the time goes:
time: 618 us; the launch traced here: 607 us
  blocking collectives  296 us (48%)
  local copies, waits for them, and re-layouts  97.6 us (16%)
  matrix products  65.2 us (11%)
  starting transfers between devices  64.2 us (10%)
  waiting for transfers between devices  45.4 us (7%)
  other arithmetic  20.7 us (3%)
  between operations  17 us (3%)
    psum x1, blocking collectives, local(): grad_level = lax.psum(level_part, ('dp', 'fx'))  154 us
    psum x1, blocking collectives, local(): lax.psum(grad_gain_local.astype(jnp.bfloat16), ('fy', 'fx'))  62.7 us
    all_gather x1, blocking collectives, local(): shard_piece = lax.all_gather(summary, 'fx', axis=1, tiled=True)  31.8 us
    reshape x8, local copies, waits for them, and re-layouts, rows_to_batch(): return tensor.reshape(tensor.shape[1], tensor.shape[2], -1, head_dim)  23 us
    another operation x7, local copies, waits for them, and re-layouts  17.7 us
    all_to_all x1, blocking collectives, local(): lax.all_to_all(to_column_groups(column_value, column_groups), 'fy', split...  13.2 us
    all_to_all x1, blocking collectives, local(): lax.all_to_all(to_row_groups(row_grad_out, row_groups), 'fx', split_axis=...  12.7 us
  transfers between devices with their start and end apart: 18, of which 7 were waited for; matrix products, arithmetic and copies ran while one was open for 27% of the time, Pallas kernels for 0%

commit v1 on v0

--- a/solution.py
+++ b/solution.py
@@ -333,7 +333,7 @@
         lambda part: part.astype(jnp.float32), lax.psum(as_sent(owned_rows), "fy")
     )
     level_part = jnp.sum(level_onehot[:, :, :, None] * grad_coarse[:, :, None, :], axis=(0, 1))
-    grad_level = lax.psum(level_part, ("dp", "fx"))
+    grad_level = jnp.sum(lax.all_gather(level_part, ("dp", "fx")), axis=0)
     summed = (
         lax.psum(grad_qkv_local.astype(jnp.bfloat16), ("fy", "fx")).astype(jnp.float32),
         lax.psum(grad_out_local.astype(jnp.bfloat16), ("fy", "fx")).astype(jnp.float32),

time: 618 us -> 596 us (0.964)
  blocking collectives: 296 us -> 225 us
  waiting for transfers between devices: 45.4 us -> 96 us
    psum x1 -> x0, blocking collectives: 154 us -> none  [local(): grad_level = lax.psum(level_part, ('dp', 'fx'))]
    all_gather x0 -> x1, blocking collectives: none -> 82.5 us  [local(): grad_level = jnp.sum(lax.all_gather(level_part, ('dp', 'fx')), axis=0)]
    psum x1, waiting for transfers between devices: 0.01 us -> 34.6 us  [local(): lax.psum(as_sent(owned_rows), 'fy')]
    psum x1, waiting for transfers between devices: 0.01 us -> 22.4 us  [local(): lax.psum(grad_qkv_local.astype(jnp.bfloat16), ('fy', 'fx'))]
    reduce_scatter x1, waiting for transfers between devices: 6.4 us -> 0.01 us  [local(): lax.psum_scatter(as_sent(dense_sum), 'fx', scatter_dimension=1, tiled=True)]
  transfers between devices with their start and end apart: 18 -> 18, of which waited for: 7 -> 8; matrix products, arithmetic and copies ran while one was open for 27% -> 28% of each run, Pallas kernels for 0% -> 0%
where the time goes in v1:
time: 596 us; the launch traced here: 584 us
  blocking collectives  225 us (38%)
  local copies, waits for them, and re-layouts  97.7 us (16%)
  waiting for transfers between devices  96 us (16%)
  matrix products  65.2 us (11%)
  starting transfers between devices  64.2 us (11%)
  other arithmetic  20.8 us (3%)
  between operations  15.1 us (3%)
    all_gather x1, blocking collectives, local(): grad_level = jnp.sum(lax.all_gather(level_part, ('dp', 'fx')), axis=0)  82.5 us
    psum x1, blocking collectives, local(): lax.psum(grad_gain_local.astype(jnp.bfloat16), ('fy', 'fx'))  63.6 us
    psum x1, waiting for transfers between devices, local(): lax.psum(as_sent(owned_rows), 'fy')  34.6 us
    all_gather x1, blocking collectives, local(): shard_piece = lax.all_gather(summary, 'fx', axis=1, tiled=True)  31.8 us
    reshape x8, local copies, waits for them, and re-layouts, rows_to_batch(): return tensor.reshape(tensor.shape[1], tensor.shape[2], -1, head_dim)  23 us
    psum x1, waiting for transfers between devices, local(): lax.psum(grad_qkv_local.astype(jnp.bfloat16), ('fy', 'fx'))  22.4 us
    another operation x7, local copies, waits for them, and re-layouts  17.7 us
    all_to_all x1, blocking collectives, local(): lax.all_to_all(to_column_groups(column_value, column_groups), 'fy', split...  13.2 us
  transfers between devices with their start and end apart: 18, of which 8 were waited for; matrix products, arithmetic and copies ran while one was open for 28% of the time, Pallas kernels for 0%

profile of v1, /device:TPU:0, one launch (start us, length us, event | category | flops | bytes accessed | tf_op | source)
XLA Modules:
  0.0 584.4 jit_solution(5938617024420577398)
XLA Ops:
  7.2 2.5 convolution_convert_fusion.1
  11.4 5.3 all-to-all-start.10
  22.5 31.8 %all_gather.9 = bf16[1,512,768]{2,1,0:T(8,128)(2,1)} all-gather(bf16[1,64,768]{2,1,0:T(8,128)(2,1)S(1)} %fusion.66), channel_id=1, replica_groups=mesh['dp'=4,'fy'=4,'fx'=8] {'fx'}, dimensions={1}, use_global_device_ids=true | all-gather | bytes 884736 | tf_op jit(solution)/shard_map/all_gather | solution.py:160
  54.3 2.8 gather_fusion
  59.7 2.8 broadcast_in_dim.39
  70.3 5.4 all-to-all-start.6
  77.5 7.2 %all-to-all-done.6 = bf16[1,16,4,8,384]{4,3,1,0,2:T(8,128)(2,1)} async-done(((bf16[1,16,4,8,384]{4,3,1,0,2:T(8,128)(2,1)}), bf16[1,16,4,8,384]{4,3,1,0,2:T(8,128)(2,1)}, u32[]{:S(2)}, u32[]{:S(2)}) %all-to-all-start.6) | async-done | bytes 393248 | tf_op jit(solution)/shard_map/all_to_all | solution.py:218
  84.7 4.1 all-to-all-start.5
  90.6 7.2 %all-to-all-done.5 = bf16[1,16,4,8,384]{4,3,1,0,2:T(8,128)(2,1)} async-done(((bf16[1,16,4,8,384]{4,3,1,0,2:T(8,128)(2,1)}), bf16[1,16,4,8,384]{4,3,1,0,2:T(8,128)(2,1)}, u32[]{:S(2)}, u32[]{:S(2)}) %all-to-all-start.5) | async-done | bytes 393248 | tf_op jit(solution)/shard_map/all_to_all | solution.py:215
  97.8 13.2 %all_to_all.270 = bf16[1,16,4,8,384]{4,3,1,0,2:T(8,128)(2,1)} all-to-all(bf16[1,16,4,8,384]{4,3,1,0,2:T(8,128)(2,1)} %copy.222), channel_id=1, replica_groups=mesh['dp'=4,'fy'=4,'fx'=8] {'fy'}, dimensions={2} | all-to-all | bytes 786432 | tf_op jit(solution)/shard_map/all_to_all | solution.py:221
  111.0 12.7 %all_to_all.271 = bf16[8,2,32,384]{3,2,1,0:T(8,128)(2,1)} all-to-all(bf16[8,2,32,384]{3,2,1,0:T(8,128)(2,1)} %bitcast.261), channel_id=1, replica_groups=mesh['dp'=4,'fy'=4,'fx'=8] {'fx'}, dimensions={0} | all-to-all | bytes 786432 | tf_op jit(solution)/shard_map/all_to_all | solution.py:246
  123.7 11.0 %all_to_all.272 = bf16[8,2,32,384]{3,2,1,0:T(8,128)(2,1)} all-to-all(bf16[8,2,32,384]{3,2,1,0:T(8,128)(2,1)S(1)} %bitcast.252), channel_id=1, replica_groups=mesh['dp'=4,'fy'=4,'fx'=8] {'fx'}, dimensions={0} | all-to-all | bytes 786432 | tf_op jit(solution)/shard_map/all_to_all | solution.py:196
  134.7 4.1 all-to-all-start.1
  138.8 2.4 reshape.396
  141.2 2.7 copy.260
  143.9 2.4 reshape.383
  146.3 2.5 reshape.385
  148.7 2.7 copy.251
  151.4 2.5 reshape.387
  153.9 2.7 copy.242
  156.6 3.3 fusion.59
  159.9 6.1 %all-to-all-start = ((bf16[8,2,32,384]{3,2,1,0:T(8,128)(2,1)}), bf16[8,2,32,384]{3,2,1,0:T(8,128)(2,1)}, u32[]{:S(2)}, u32[]{:S(2)}) async-start(bf16[8,2,32,384]{3,2,1,0:T(8,128)(2,1)} %bitcast.250), calls=%async_computation | async-start | bytes 786432 | tf_op jit(solution)/shard_map/all_to_all | solution.py:199
  166.0 4.0 fusion.89
  170.0 4.6 fusion.37
  174.6 2.2 copy.244
  176.8 4.1 all-to-all-start.11
  180.9 3.0 convolution_convert_fusion.2
  184.0 2.2 copy.262
  186.2 4.6 fusion.40
  190.8 2.2 copy.253
  193.1 2.7 copy.283
  195.8 3.0 reshape.450
  198.8 2.7 copy.279
  201.5 3.0 reshape.447
  204.6 2.7 copy.280
  207.3 3.0 reshape.448
  210.3 2.7 copy.281
  213.1 3.0 reshape.449
  216.1 4.8 all-to-all-start.13
  220.8 4.5 fusion.90
  225.4 4.5 all-to-all-done.13
  229.9 4.1 all-to-all-start.15
  234.0 3.3 convolution_convert_fusion.4
  239.2 3.7 all-to-all-done.15
  243.0 5.9 %all-to-all-start.14 = ((bf16[1,2,256,384]{3,1,0,2:T(2,128)(2,1)}), bf16[1,2,256,384]{3,1,0,2:T(2,128)(2,1)}, u32[]{:S(2)}, u32[]{:S(2)}) async-start(bf16[1,2,256,384]{3,1,0,2:T(2,128)(2,1)} %copy.257), calls=%async_computation.14 | async-start | bytes 786432 | tf_op jit(solution)/shard_map/all_to_all | solution.py:262
  248.9 3.4 fusion.91
  252.3 6.6 %fusion.43 = bf16[2,6,64,256]{3,2,1,0:T(8,128)(2,1)} fusion(bf16[2,256,6,64]{1,3,2,0:T(8,128)(2,1)} %reshape.449, f32[2,6,256,256]{2,3,1,0:T(8,128)} %fusion.91, f32[2,6,256,256]{2,3,1,0:T(8,128)} %get-tuple-element.28, f32[2,6,256]{2,1,0:T(8,128)} %get-tuple-element.27), kind=kOutput, calls=%fused_computation.49 | convolution fusion | flops 106368256 | bytes 7090176 | tf_op jit(solution)/shard_map/bhqk,bkhd->bqhd/dot_general | solution.py:64
  260.8 5.7 all-to-all-start.9
  266.5 6.6 %fusion.46 = bf16[2,6,64,256]{3,2,1,0:T(8,128)(2,1)} fusion(bf16[2,256,6,64]{1,3,2,0:T(8,128)(2,1)} %reshape.448, f32[2,6,256,256]{2,3,1,0:T(8,128)} %fusion.91, f32[2,6,256,256]{2,3,1,0:T(8,128)} %get-tuple-element.28, f32[2,6,256]{2,1,0:T(8,128)} %get-tuple-element.27), kind=kOutput, calls=%fused_computation.50 | convolution fusion | flops 106368256 | bytes 7090176 | tf_op jit(solution)/shard_map/bhqk,bqhd->bkhd/dot_general | solution.py:70
  275.1 5.7 all-to-all-start.12
  295.0 2.2 fusion.22
  306.5 3.5 all-to-all-start.7
  310.0 2.3 convolution_convert_fusion.5
  313.4 6.9 %all-to-all-done.7 = bf16[1,64,1,8,384]{4,3,2,0,1:T(8,128)(2,1)S(1)} async-done(((bf16[1,64,1,8,384]{4,3,2,0,1:T(8,128)(2,1)}), bf16[1,64,1,8,384]{4,3,2,0,1:T(8,128)(2,1)S(1)}, u32[]{:S(2)}, u32[]{:S(2)}) %all-to-all-start.7) | async-done | bytes 393248 | tf_op jit(solution)/shard_map/all_to_all | solution.py:233
  320.3 5.1 all-to-all-start.3
  325.5 9.3 %all-to-all-done.3 = bf16[1,2,256,384]{3,1,0,2:T(2,128)(2,1)S(1)} async-done(((bf16[1,2,256,384]{3,1,0,2:T(2,128)(2,1)}), bf16[1,2,256,384]{3,1,0,2:T(2,128)(2,1)S(1)}, u32[]{:S(2)}, u32[]{:S(2)}) %all-to-all-start.3) | async-done | bytes 393248 | tf_op jit(solution)/shard_map/all_to_all | solution.py:211
  345.2 5.5 bitcast_convert_fusion
  352.5 10.5 %all-reduce = bf16[768]{0:T(1024)(128)(2,1)S(1)} all-reduce(bf16[768]{0:T(1024)(128)(2,1)S(1)} %get-tuple-element.7), channel_id=6, replica_groups=mesh['dp'=4,'fy'=4,'fx'=8] {'dp'}, use_global_device_ids=true, to_apply=%region_19.20.clone | all-reduce | flops 768 | bytes 3072
  363.1 63.6 %psum.34 = bf16[192]{0:T(256)(128)(2,1)S(1)} all-reduce(bf16[192]{0:T(256)(128)(2,1)S(1)} %dynamic-slice.1), channel_id=1, replica_groups=mesh['dp'=4,'fy'=4,'fx'=8] {'fy','fx'}, use_global_device_ids=true, to_apply=%region_18.19 | all-reduce | flops 192 | bytes 768 | tf_op jit(solution)/shard_map/psum | solution.py:340
  426.7 2.9 fusion.23
  430.3 34.6 %all-reduce.5.cloned.1.call-done = bf16[1,64,768]{2,1,0:T(8,128)(2,1)} async-done(((bf16[1,64,768]{2,1,0:T(8,128)(2,1)}), bf16[1,64,768]{2,1,0:T(8,128)(2,1)}) %all-reduce.5.cloned.1.call-update) | async-done | bytes 98320 | tf_op jit(solution)/shard_map/psum | solution.py:333
  466.0 82.5 %all-gather.1 = f32[32,3,768]{2,1,0:T(4,128)S(1)} all-gather(f32[1,3,768]{2,1,0:T(4,128)S(1)} %bitcast.281), channel_id=2, replica_groups=mesh['dp'=4,'fy'=4,'fx'=8] {'dp','fx'}, dimensions={0}, use_global_device_ids=true | all-gather | bytes 304128 | tf_op jit(solution)/shard_map/all_gather | solution.py:336
  550.8 22.4 %all-reduce.7.cloned.1.call-done = (bf16[192,2304]{1,0:T(8,128)(2,1)}, bf16[192,768]{1,0:T(8,128)(2,1)}) async-done(((bf16[192,2304]{1,0:T(8,128)(2,1)}, bf16[192,768]{1,0:T(8,128)(2,1)}), (bf16[192,2304]{1,0:T(8,128)(2,1)}, bf16[192,768]{1,0:T(8,128)(2,1)})) %all-reduce.7.cloned.1.call-update) | async-done | bytes 1179664 | tf_op jit(solution)/shard_map/psum | solution.py:338
  575.1 2.5 convert_multiply_fusion
  (154 shorter events, 69.5 us)
Async XLA Ops:
  7.2 59.0 %copy-start = (bf16[768,2304]{1,0:T(8,128)(2,1)S(1)}, bf16[768,2304]{1,0:T(8,128)(2,1)}, u32[]{:S(2)}) copy-start(bf16[768,2304]{1,0:T(8,128)(2,1)} %param.15) | copy-start | bytes 10616836
  9.7 7.0 %copy-start.23 = (s32[1,16,8]{1,2,0:T(8,128)S(1)}, s32[1,16,8]{1,2,0:T(8,128)}, u32[]{:S(2)}) copy-start(s32[1,16,8]{1,2,0:T(8,128)} %param.10) | copy-start | bytes 1540
  9.7 7.5 %copy-start.27 = (s32[1,64]{1,0:T(1,128)S(1)}, s32[1,64]{1,0:T(1,128)}, u32[]{:S(2)}) copy-start(s32[1,64]{1,0:T(1,128)} %param.12) | copy-start | bytes 772
  11.4 58.9 %all-to-all-start.10 = ((bf16[1,16,4,8,384]{4,3,1,0,2:T(8,128)(2,1)}), bf16[1,16,4,8,384]{4,3,1,0,2:T(8,128)(2,1)}, u32[]{:S(2)}, u32[]{:S(2)}) async-start(bf16[1,16,4,8,384]{4,3,1,0,2:T(8,128)(2,1)} %copy.239), calls=%async_computation.10 | async-start | bytes 786432 | tf_op jit(solution)/shard_map/all_to_all | solution.py:273
  62.4 2.1 copy-start.2
  62.5 2.3 copy-start.12
  62.5 2.3 copy-start.25
  66.2 2.0 copy-start.21
  70.3 14.4 %all-to-all-start.6 = ((bf16[1,16,4,8,384]{4,3,1,0,2:T(8,128)(2,1)}), bf16[1,16,4,8,384]{4,3,1,0,2:T(8,128)(2,1)}, u32[]{:S(2)}, u32[]{:S(2)}) async-start(bf16[1,16,4,8,384]{4,3,1,0,2:T(8,128)(2,1)} %copy.224), calls=%async_computation.6 | async-start | bytes 786432 | tf_op jit(solution)/shard_map/all_to_all | solution.py:218
  84.7 13.1 %all-to-all-start.5 = ((bf16[1,16,4,8,384]{4,3,1,0,2:T(8,128)(2,1)}), bf16[1,16,4,8,384]{4,3,1,0,2:T(8,128)(2,1)}, u32[]{:S(2)}, u32[]{:S(2)}) async-start(bf16[1,16,4,8,384]{4,3,1,0,2:T(8,128)(2,1)} %copy.223), calls=%async_computation.5 | async-start | bytes 786432 | tf_op jit(solution)/shard_map/all_to_all | solution.py:215
  97.8 25.9 %copy-start.14 = (bf16[1,16,32,384]{3,2,1,0:T(8,128)(2,1)S(1)}, bf16[1,16,32,384]{3,2,1,0:T(8,128)(2,1)}, u32[]{:S(2)}) copy-start(bf16[1,16,32,384]{3,2,1,0:T(8,128)(2,1)} %get-tuple-element.15) | copy-start | bytes 1179652
  134.7 25.2 %all-to-all-start.1 = ((bf16[8,2,32,384]{3,2,1,0:T(8,128)(2,1)}), bf16[8,2,32,384]{3,2,1,0:T(8,128)(2,1)}, u32[]{:S(2)}, u32[]{:S(2)}) async-start(bf16[8,2,32,384]{3,2,1,0:T(8,128)(2,1)} %bitcast.251), calls=%async_computation.1 | async-start | bytes 786432 | tf_op jit(solution)/shard_map/all_to_all | solution.py:193
  159.9 16.9 %all-to-all-start = ((bf16[8,2,32,384]{3,2,1,0:T(8,128)(2,1)}), bf16[8,2,32,384]{3,2,1,0:T(8,128)(2,1)}, u32[]{:S(2)}, u32[]{:S(2)}) async-start(bf16[8,2,32,384]{3,2,1,0:T(8,128)(2,1)} %bitcast.250), calls=%async_computation | async-start | bytes 786432 | tf_op jit(solution)/shard_map/all_to_all | solution.py:199
  176.8 39.3 %all-to-all-start.11 = ((bf16[1,64,1,8,384]{4,3,2,0,1:T(8,128)(2,1)}), bf16[1,64,1,8,384]{4,3,2,0,1:T(8,128)(2,1)}, u32[]{:S(2)}, u32[]{:S(2)}) async-start(bf16[1,64,1,8,384]{4,3,2,0,1:T(8,128)(2,1)} %copy.244), calls=%async_computation.11 | async-start | bytes 786432 | tf_op jit(solution)/shard_map/all_to_all | solution.py:291
  216.1 13.8 %all-to-all-start.13 = ((bf16[1,64,1,8,384]{4,3,2,0,1:T(8,128)(2,1)}), bf16[1,64,1,8,384]{4,3,2,0,1:T(8,128)(2,1)}, u32[]{:S(2)}, u32[]{:S(2)}) async-start(bf16[1,64,1,8,384]{4,3,2,0,1:T(8,128)(2,1)} %copy.253), calls=%async_computation.13 | async-start | bytes 786432 | tf_op jit(solution)/shard_map/all_to_all | solution.py:292
  229.9 13.1 %all-to-all-start.15 = ((bf16[1,64,1,8,384]{4,3,2,0,1:T(8,128)(2,1)}), bf16[1,64,1,8,384]{4,3,2,0,1:T(8,128)(2,1)}, u32[]{:S(2)}, u32[]{:S(2)}) async-start(bf16[1,64,1,8,384]{4,3,2,0,1:T(8,128)(2,1)} %copy.262), calls=%async_computation.15 | async-start | bytes 786432 | tf_op jit(solution)/shard_map/all_to_all | solution.py:293
  243.0 17.9 %all-to-all-start.14 = ((bf16[1,2,256,384]{3,1,0,2:T(2,128)(2,1)}), bf16[1,2,256,384]{3,1,0,2:T(2,128)(2,1)}, u32[]{:S(2)}, u32[]{:S(2)}) async-start(bf16[1,2,256,384]{3,1,0,2:T(2,128)(2,1)} %copy.257), calls=%async_computation.14 | async-start | bytes 786432 | tf_op jit(solution)/shard_map/all_to_all | solution.py:262
  260.8 14.2 %all-to-all-start.9 = ((bf16[1,2,256,384]{3,1,0,2:T(2,128)(2,1)}), bf16[1,2,256,384]{3,1,0,2:T(2,128)(2,1)}, u32[]{:S(2)}, u32[]{:S(2)}) async-start(bf16[1,2,256,384]{3,1,0,2:T(2,128)(2,1)} %copy.236), calls=%async_computation.9 | async-start | bytes 786432 | tf_op jit(solution)/shard_map/all_to_all | solution.py:260
  275.1 16.9 %all-to-all-start.12 = ((bf16[1,2,256,384]{3,1,0,2:T(2,128)(2,1)}), bf16[1,2,256,384]{3,1,0,2:T(2,128)(2,1)}, u32[]{:S(2)}, u32[]{:S(2)}) async-start(bf16[1,2,256,384]{3,1,0,2:T(2,128)(2,1)} %copy.248), calls=%async_computation.12 | async-start | bytes 786432 | tf_op jit(solution)/shard_map/all_to_all | solution.py:261
  280.8 148.9 %reduce-scatter.4.cloned.1.call-start = ((), (), s32[]{:S(2)}) async-start(), calls=%async_computation.19 | async-start | bytes 884736 | tf_op jit(solution)/shard_map/reduce_scatter | solution.py:330
  291.9 1.2 copy-start.9
  291.9 1.3 copy-start.17
  293.0 1.1 copy-start.16
  293.1 1.1 copy-start.7
  293.1 1.2 copy-start.5
  293.2 1.2 copy-start.15
  293.3 1.7 copy-start.4
  293.3 1.7 copy-start.26
  295.0 2.2 copy-start.19
  301.8 1.5 copy-start.11
  301.8 1.5 copy-start.24
  305.4 4.6 copy-start.18
  305.4 4.6 copy-start.29
  306.5 13.8 %all-to-all-start.7 = ((bf16[1,64,1,8,384]{4,3,2,0,1:T(8,128)(2,1)}), bf16[1,64,1,8,384]{4,3,2,0,1:T(8,128)(2,1)S(1)}, u32[]{:S(2)}, u32[]{:S(2)}) async-start(bf16[1,64,1,8,384]{4,3,2,0,1:T(8,128)(2,1)} %copy.229), calls=%async_computation.7 | async-start | bytes 786432 | tf_op jit(solution)/shard_map/all_to_all | solution.py:233
  313.4 21.5 %copy-start.10 = (bf16[8,1,2,32,384]{4,3,2,0,1:T(8,128)(2,1)S(1)}, bf16[8,1,2,32,384]{4,3,2,0,1:T(8,128)(2,1)}, u32[]{:S(2)}) copy-start(bf16[8,1,2,32,384]{4,3,2,0,1:T(8,128)(2,1)} %copy.238) | copy-start | bytes 1179652
  320.3 14.5 %all-to-all-start.3 = ((bf16[1,2,256,384]{3,1,0,2:T(2,128)(2,1)}), bf16[1,2,256,384]{3,1,0,2:T(2,128)(2,1)S(1)}, u32[]{:S(2)}, u32[]{:S(2)}) async-start(bf16[1,2,256,384]{3,1,0,2:T(2,128)(2,1)} %copy.219), calls=%async_computation.3 | async-start | bytes 786432 | tf_op jit(solution)/shard_map/all_to_all | solution.py:211
  325.4 104.9 %reduce-scatter.8.cloned.1.call-start = ((), (), s32[]{:S(2)}) async-start(), calls=%async_computation.22 | async-start | bytes 1474560 | tf_op jit(solution)/shard_map/reduce_scatter | solution.py:346
  325.5 10.4 %copy-start.20 = (bf16[1,16,32,768]{3,2,1,0:T(8,128)(2,1)S(1)}, bf16[1,16,32,768]{3,2,1,0:T(8,128)(2,1)}, u32[]{:S(2)}) copy-start(bf16[1,16,32,768]{3,2,1,0:T(8,128)(2,1)} %param.17) | copy-start | bytes 2359300
  337.7 2.1 copy-start.8
  337.7 4.8 copy-start.6
  337.7 92.6 %reduce-scatter.6.cloned.1.call-start = ((), (), s32[]{:S(2)}) async-start(), calls=%async_computation.21 | async-start | bytes 4423680 | tf_op jit(solution)/shard_map/reduce_scatter | solution.py:343
  339.8 5.3 copy-start.22
  350.6 0.7 copy-start.28
  350.6 76.1 %copy-start.3 = (f32[1,16,32,768]{3,2,1,0:T(8,128)S(1)}, f32[1,16,32,768]{3,2,1,0:T(8,128)}, u32[]{:S(2)}) copy-start(f32[1,16,32,768]{3,2,1,0:T(8,128)} %broadcast_in_dim.39) | copy-start | bytes 4718596
  350.6 76.1 %copy-start.13 = (bf16[1,16,32,768]{3,2,1,0:T(8,128)(2,1)S(1)}, bf16[1,16,32,768]{3,2,1,0:T(8,128)(2,1)}, u32[]{:S(2)}) copy-start(bf16[1,16,32,768]{3,2,1,0:T(8,128)(2,1)} %param.9) | copy-start | bytes 2359300
  350.6 114.3 %all-reduce.5.cloned.1.call-start = ((), (), s32[]{:S(2)}) async-start(), calls=%async_computation.20 | async-start | bytes 196608 | tf_op jit(solution)/shard_map/psum | solution.py:333
  429.7 143.5 %all-reduce.7.cloned.1.call-start = ((), (), s32[]{:S(2)}) async-start(), calls=%async_computation.23 | async-start | bytes 2359296 | tf_op jit(solution)/shard_map/psum | solution.py:338
  573.2 4.5 copy-start.1
Sparse Core Ops, SparseCore 0:
  302.9 40.2 reduce-scatter.3
  346.2 23.0 reduce-scatter.7
  371.8 41.1 reduce-scatter.5
  429.8 35.0 all-reduce.4
  468.1 104.9 all-reduce.6
